TPU v7x, 128 devices: a whole 4x4x4 slice. The times are simulated.
128 devices in a mesh: req: 32 (over x, z, core), tp: 4 (over y).
Axes of the slice: x: 4, y: 4, z: 4, core: 2. Of those that a mesh axis runs over, the one named last changes fastest.
Arguments:
- hidden_states: bfloat16 [8192, 2048], P('req'), may hold values from -30 to 30
- norm_gain: float32 [2048], replicated, may hold values from 0.5 to 1.5
- head: bfloat16 [2048, 98304], P(None, ('req', 'tp')), may hold values from -1 to 1
- target_ids: int32 [8192], P('req'), may hold values from 0 to 98303
- lengths: int32 [32], P('req'), may hold values from 32 to 256, as said below
Outputs:
- token_logprob: float32 [8192], P('req')
- token_entropy: float32 [8192], P('req')
- seq_mean_logprob: float32 [32], P('req')
- seq_top_logit: float32 [32], P('req')
Inputs may be any that keep to these rules, and one draw needn't show every extreme that they name: `lengths`: each completion has at least 32 and at most 256 live slots; some completion has exactly 256.
All inputs are finite; a program needn't handle non-finite values.
Results may differ from a plain program's by a relative error of at most 0.0018.
Values may be sent and summed in bfloat16 or wider, within the bound.
A program may use at most 128 MiB of HBM per device.

v0:
```python
import math
import jax
import jax.numpy as jnp
from jax import lax
from jax.sharding import PartitionSpec as P


def combined_all(value, axis, combine):
    everything = jax.tree.map(lambda part: lax.all_gather(part, axis), value)
    leading = jax.tree.map(lambda part: part[0], everything)

    def turn(k, so_far):
        return combine(so_far, jax.tree.map(lambda part: part[k], everything))

    return lax.fori_loop(1, lax.axis_size(axis), turn, leading)


def combine(first, second):
    top = jnp.maximum(first[0], second[0])
    left = jnp.exp(first[0] - top)
    right = jnp.exp(second[0] - top)
    return (
        top,
        first[1] * left + second[1] * right,
        first[2] * left + second[2] * right,
        first[3] + second[3],
    )


def block_stats(block, target, matrix, vocab_ids):
    logits = jnp.dot(block, matrix, preferred_element_type=jnp.float32)
    top = jnp.max(logits, axis=-1)
    shifted = jnp.exp(logits - top[:, None])
    weight_sum = jnp.sum(shifted, axis=-1)
    weighted = jnp.sum(shifted * logits, axis=-1)
    hit = vocab_ids == target[:, None]
    picked = jnp.sum(jnp.where(hit, logits, 0.0), axis=-1)
    return (top, weight_sum, weighted, picked)


def blocked_stats(block, target, matrix, vocab_ids):
    count = block.shape[0]
    step = math.gcd(count, 512)
    stats = lax.map(
        lambda a: block_stats(a[0], a[1], matrix, vocab_ids),
        (block.reshape(count // step, step, block.shape[1]), target.reshape(count // step, step)),
    )
    return tuple((s.reshape(-1) for s in stats))


def per_device(hidden_states, norm_gain, head, target_ids, lengths):
    feats = hidden_states.astype(jnp.float32)
    scale = lax.rsqrt(jnp.mean(feats * feats, axis=-1, keepdims=True) + 1e-06)
    normed = (feats * scale * norm_gain).astype(jnp.bfloat16)
    rows = hidden_states.shape[0]
    vdev = head.shape[1]
    n_req = lax.axis_size("req")
    n_tp = lax.axis_size("tp")
    my_req = lax.axis_index("req")
    vbase = (my_req * n_tp + lax.axis_index("tp")) * vdev
    columns = lax.broadcasted_iota(jnp.int32, (1, vdev), 1)
    own_vocab = columns + vbase
    block = lax.all_gather(normed, "req", axis=0, tiled=True)
    target = lax.all_gather(target_ids, "req", axis=0, tiled=True)
    stats = blocked_stats(block, target, head, own_vocab)
    gathered = tuple((new for new in stats))
    shaped = tuple((s.reshape(n_req, rows) for s in gathered))
    arrived = (
        lax.all_to_all(shaped[0], "req", split_axis=0, concat_axis=0, tiled=True),
        lax.all_to_all(shaped[1], "req", split_axis=0, concat_axis=0, tiled=True),
        lax.all_to_all(shaped[2], "req", split_axis=0, concat_axis=0, tiled=True),
        lax.all_to_all(shaped[3], "req", split_axis=0, concat_axis=0, tiled=True),
    )
    top = jnp.max(arrived[0], axis=0)
    factor = jnp.exp(arrived[0] - top[None, :])
    own = (
        top,
        jnp.sum(arrived[1] * factor, axis=0),
        jnp.sum(arrived[2] * factor, axis=0),
        jnp.sum(arrived[3], axis=0),
    )
    merged = combined_all((own[0], own[1], own[2], own[3]), "tp", combine)
    top, weight_sum, weighted, picked = merged
    log_norm = top + jnp.log(weight_sum)
    live = jnp.arange(rows, dtype=jnp.int32) < lengths[0]
    logprob = jnp.where(live, picked - log_norm, jnp.float32(0.0))
    entropy = jnp.where(live, log_norm - weighted / weight_sum, jnp.float32(0.0))
    mean_lp = (jnp.sum(logprob) / lengths[0].astype(jnp.float32)).reshape(1)
    top_live = jnp.max(jnp.where(live, top, jnp.float32(-1e30))).reshape(1)
    return (logprob, entropy, mean_lp, top_live)


def solution(mesh):
    in_specs = (P("req", None), P(), P(None, ("req", "tp")), P("req"), P("req"))
    out_specs = (P("req"), P("req"), P("req"), P("req"))
    return jax.shard_map(
        per_device, mesh=mesh, in_specs=in_specs, out_specs=out_specs, check_vma=False
    )
```

profile of v0, /device:TPU:14, one launch (start us, length us, event | category | flops | bytes accessed | tf_op | source)
XLA Modules:
  0.0 283.6 jit_solution(8951670508299853403)
XLA Ops:
  11.5 25.2 %all-gather.4 = s32[32,1,256]{2,1,0:T(1,128)S(1)} all-gather(s32[1,1,256]{2,1,0:T(1,128)S(1)} %bitcast.102), channel_id=1, replica_groups=mesh['req'=32,'tp'=4] {'req'}, dimensions={0}, use_global_device_ids=true | all-gather | bytes 33792 | tf_op jit(solution)/shard_map/all_gather | solution.py:64
  36.8 91.0 %all-gather.11.cloned.1.call-done = bf16[8192,2048]{1,0:T(8,128)(2,1)} async-done(((bf16[256,2048]{1,0:T(8,128)(2,1)}), bf16[8192,2048]{1,0:T(8,128)(2,1)}) %all-gather.11.cloned.1.call-update) | async-done | bytes 33554448 | tf_op jit(solution)/shard_map/all_gather | solution.py:63
  127.8 72.3 %while.39 = (s32[]{:T(128)}, f32[16,512]{1,0:T(8,128)S(1)}, f32[16,512]{1,0:T(8,128)S(1)}, f32[16,512]{1,0:T(8,128)S(1)}, f32[16,512]{1,0:T(8,128)S(1)}, /*index...) while((s32[]{:T(128)}, f32[16,512]{1,0:T(8,128)S(1)}, ...), condition=%wide.region_6.7_spmd.clone, body=%wide.region_1.6_spmd.clone.sunk | while | flops 1613757184 | bytes 8428165 | solution.py:44
  132.3 3.5 %fusion.19 = (f32[512]{0:T(512)S(1)}, f32[512,768]{1,0:T(8,128)S(1)}) fusion(bf16[2048,768]{1,0:T(8,128)(2,1)S(1)} %get-tuple-element.519, bf16[16,512,2048]{2,1,0:T(8,128)(2,1)} %get-tuple-element.518, s32[]{:T(128)} %get-tuple-element.502), kind=kOutput, calls=%fused_computation.41.clone.1 | convolution fusion | flops 1611005440 | bytes 6818304 | tf_op jit(solution)/shard_map/while/body/eval_jaxpr/dot_general | solution.py:31
  136.8 3.5 %fusion.19 = (f32[512]{0:T(512)S(1)}, f32[512,768]{1,0:T(8,128)S(1)}) fusion(bf16[2048,768]{1,0:T(8,128)(2,1)S(1)} %get-tuple-element.519, bf16[16,512,2048]{2,1,0:T(8,128)(2,1)} %get-tuple-element.518, s32[]{:T(128)} %get-tuple-element.502), kind=kOutput, calls=%fused_computation.41.clone.1 | convolution fusion | flops 1611005440 | bytes 6818304 | tf_op jit(solution)/shard_map/while/body/eval_jaxpr/dot_general | solution.py:31
  141.4 3.5 %fusion.19 = (f32[512]{0:T(512)S(1)}, f32[512,768]{1,0:T(8,128)S(1)}) fusion(bf16[2048,768]{1,0:T(8,128)(2,1)S(1)} %get-tuple-element.519, bf16[16,512,2048]{2,1,0:T(8,128)(2,1)} %get-tuple-element.518, s32[]{:T(128)} %get-tuple-element.502), kind=kOutput, calls=%fused_computation.41.clone.1 | convolution fusion | flops 1611005440 | bytes 6818304 | tf_op jit(solution)/shard_map/while/body/eval_jaxpr/dot_general | solution.py:31
  150.4 3.5 %fusion.19 = (f32[512]{0:T(512)S(1)}, f32[512,768]{1,0:T(8,128)S(1)}) fusion(bf16[2048,768]{1,0:T(8,128)(2,1)S(1)} %get-tuple-element.519, bf16[16,512,2048]{2,1,0:T(8,128)(2,1)} %get-tuple-element.518, s32[]{:T(128)} %get-tuple-element.502), kind=kOutput, calls=%fused_computation.41.clone.1 | convolution fusion | flops 1611005440 | bytes 6818304 | tf_op jit(solution)/shard_map/while/body/eval_jaxpr/dot_general | solution.py:31
  159.4 3.5 %fusion.19 = (f32[512]{0:T(512)S(1)}, f32[512,768]{1,0:T(8,128)S(1)}) fusion(bf16[2048,768]{1,0:T(8,128)(2,1)S(1)} %get-tuple-element.519, bf16[16,512,2048]{2,1,0:T(8,128)(2,1)} %get-tuple-element.518, s32[]{:T(128)} %get-tuple-element.502), kind=kOutput, calls=%fused_computation.41.clone.1 | convolution fusion | flops 1611005440 | bytes 6818304 | tf_op jit(solution)/shard_map/while/body/eval_jaxpr/dot_general | solution.py:31
  164.0 3.5 %fusion.19 = (f32[512]{0:T(512)S(1)}, f32[512,768]{1,0:T(8,128)S(1)}) fusion(bf16[2048,768]{1,0:T(8,128)(2,1)S(1)} %get-tuple-element.519, bf16[16,512,2048]{2,1,0:T(8,128)(2,1)} %get-tuple-element.518, s32[]{:T(128)} %get-tuple-element.502), kind=kOutput, calls=%fused_computation.41.clone.1 | convolution fusion | flops 1611005440 | bytes 6818304 | tf_op jit(solution)/shard_map/while/body/eval_jaxpr/dot_general | solution.py:31
  168.5 3.5 %fusion.19 = (f32[512]{0:T(512)S(1)}, f32[512,768]{1,0:T(8,128)S(1)}) fusion(bf16[2048,768]{1,0:T(8,128)(2,1)S(1)} %get-tuple-element.519, bf16[16,512,2048]{2,1,0:T(8,128)(2,1)} %get-tuple-element.518, s32[]{:T(128)} %get-tuple-element.502), kind=kOutput, calls=%fused_computation.41.clone.1 | convolution fusion | flops 1611005440 | bytes 6818304 | tf_op jit(solution)/shard_map/while/body/eval_jaxpr/dot_general | solution.py:31
  186.6 3.5 %fusion.19 = (f32[512]{0:T(512)S(1)}, f32[512,768]{1,0:T(8,128)S(1)}) fusion(bf16[2048,768]{1,0:T(8,128)(2,1)S(1)} %get-tuple-element.519, bf16[16,512,2048]{2,1,0:T(8,128)(2,1)} %get-tuple-element.518, s32[]{:T(128)} %get-tuple-element.502), kind=kOutput, calls=%fused_computation.41.clone.1 | convolution fusion | flops 1611005440 | bytes 6818304 | tf_op jit(solution)/shard_map/while/body/eval_jaxpr/dot_general | solution.py:31
  191.1 3.5 %fusion.19 = (f32[512]{0:T(512)S(1)}, f32[512,768]{1,0:T(8,128)S(1)}) fusion(bf16[2048,768]{1,0:T(8,128)(2,1)S(1)} %get-tuple-element.519, bf16[16,512,2048]{2,1,0:T(8,128)(2,1)} %get-tuple-element.518, s32[]{:T(128)} %get-tuple-element.502), kind=kOutput, calls=%fused_computation.41.clone.1 | convolution fusion | flops 1611005440 | bytes 6818304 | tf_op jit(solution)/shard_map/while/body/eval_jaxpr/dot_general | solution.py:31
  195.6 3.5 %fusion.19 = (f32[512]{0:T(512)S(1)}, f32[512,768]{1,0:T(8,128)S(1)}) fusion(bf16[2048,768]{1,0:T(8,128)(2,1)S(1)} %get-tuple-element.519, bf16[16,512,2048]{2,1,0:T(8,128)(2,1)} %get-tuple-element.518, s32[]{:T(128)} %get-tuple-element.502), kind=kOutput, calls=%fused_computation.41.clone.1 | convolution fusion | flops 1611005440 | bytes 6818304 | tf_op jit(solution)/shard_map/while/body/eval_jaxpr/dot_general | solution.py:31
  200.8 5.6 %all-to-all-start = ((f32[32,1,256]{2,1,0:T(1,128)}), f32[32,1,256]{2,1,0:T(1,128)S(1)}, u32[]{:S(2)}, u32[]{:S(2)}) async-start(f32[32,1,256]{2,1,0:T(1,128)} %all_to_all.30), calls=%async_computation | async-start | bytes 65536 | tf_op jit(solution)/shard_map/all_to_all | solution.py:69
  207.0 4.9 %all-to-all-done = f32[32,1,256]{2,1,0:T(1,128)S(1)} async-done(((f32[32,1,256]{2,1,0:T(1,128)}), f32[32,1,256]{2,1,0:T(1,128)S(1)}, u32[]{:S(2)}, u32[]{:S(2)}) %all-to-all-start) | async-done | bytes 32800 | tf_op jit(solution)/shard_map/all_to_all | solution.py:69
  211.9 5.7 %all-to-all-start.1 = ((f32[32,1,256]{2,1,0:T(1,128)}), f32[32,1,256]{2,1,0:T(1,128)S(1)}, u32[]{:S(2)}, u32[]{:S(2)}) async-start(f32[32,1,256]{2,1,0:T(1,128)} %all_to_all.32), calls=%async_computation.1 | async-start | bytes 65536 | tf_op jit(solution)/shard_map/all_to_all | solution.py:70
  218.2 4.8 %all-to-all-done.1 = f32[32,1,256]{2,1,0:T(1,128)S(1)} async-done(((f32[32,1,256]{2,1,0:T(1,128)}), f32[32,1,256]{2,1,0:T(1,128)S(1)}, u32[]{:S(2)}, u32[]{:S(2)}) %all-to-all-start.1) | async-done | bytes 32800 | tf_op jit(solution)/shard_map/all_to_all | solution.py:70
  223.1 5.8 %all-to-all-start.2 = ((f32[32,1,256]{2,1,0:T(1,128)}), f32[32,1,256]{2,1,0:T(1,128)S(1)}, u32[]{:S(2)}, u32[]{:S(2)}) async-start(f32[32,1,256]{2,1,0:T(1,128)} %all_to_all.36), calls=%async_computation.2 | async-start | bytes 65536 | tf_op jit(solution)/shard_map/all_to_all | solution.py:71
  230.2 4.1 %all-to-all-done.2 = f32[32,1,256]{2,1,0:T(1,128)S(1)} async-done(((f32[32,1,256]{2,1,0:T(1,128)}), f32[32,1,256]{2,1,0:T(1,128)S(1)}, u32[]{:S(2)}, u32[]{:S(2)}) %all-to-all-start.2) | async-done | bytes 32800 | tf_op jit(solution)/shard_map/all_to_all | solution.py:71
  234.4 5.8 %all-to-all-start.3 = ((f32[32,1,256]{2,1,0:T(1,128)}), f32[32,1,256]{2,1,0:T(1,128)S(1)}, u32[]{:S(2)}, u32[]{:S(2)}) async-start(f32[32,1,256]{2,1,0:T(1,128)} %all_to_all.39), calls=%async_computation.3 | async-start | bytes 65536 | tf_op jit(solution)/shard_map/all_to_all | solution.py:72
  240.2 7.8 %all-gather.6 = f32[4,1,256]{2,1,0:T(1,128)S(1)} all-gather(f32[1,1,256]{2,1,0:T(1,128)S(1)} %bitcast.100), channel_id=3, replica_groups=mesh['req'=32,'tp'=4] {'tp'}, dimensions={0}, use_global_device_ids=true | all-gather | bytes 5120 | tf_op jit(solution)/shard_map/all_gather | solution.py:9
  248.0 9.4 %all-gather.7 = f32[4,1,256]{2,1,0:T(1,128)S(1)} all-gather(f32[1,1,256]{2,1,0:T(1,128)S(1)} %bitcast.99), channel_id=4, replica_groups=mesh['req'=32,'tp'=4] {'tp'}, dimensions={0}, use_global_device_ids=true | all-gather | bytes 5120 | tf_op jit(solution)/shard_map/all_gather | solution.py:9
  257.4 7.0 %all-gather.5 = f32[4,1,256]{2,1,0:T(1,128)S(1)} all-gather(f32[1,1,256]{2,1,0:T(1,128)S(1)} %bitcast.98), channel_id=2, replica_groups=mesh['req'=32,'tp'=4] {'tp'}, dimensions={0}, use_global_device_ids=true | all-gather | bytes 5120 | tf_op jit(solution)/shard_map/all_gather | solution.py:9
  264.4 9.0 %all-gather.8 = f32[4,1,256]{2,1,0:T(1,128)S(1)} all-gather(f32[1,1,256]{2,1,0:T(1,128)S(1)} %bitcast.101), channel_id=5, replica_groups=mesh['req'=32,'tp'=4] {'tp'}, dimensions={0}, use_global_device_ids=true | all-gather | bytes 5120 | tf_op jit(solution)/shard_map/all_gather | solution.py:9
  (169 shorter events, 45.5 us)
Async XLA Ops:
  7.2 4.3 %copy-start = (s32[256]{0:T(256)S(1)}, s32[256]{0:T(256)}, u32[]{:S(2)}) copy-start(s32[256]{0:T(256)} %param.12) | copy-start | bytes 3076
  7.2 120.6 %copy-start.1 = (bf16[2048,768]{1,0:T(8,128)(2,1)S(1)}, bf16[2048,768]{1,0:T(8,128)(2,1)}, u32[]{:S(2)}) copy-start(bf16[2048,768]{1,0:T(8,128)(2,1)} %param.11) | copy-start | bytes 9437188
  7.2 120.6 %all-gather.11.cloned.1.call-start = ((), (), s32[]{:S(2)}) async-start(), calls=%async_computation.4 | async-start | bytes 34603008 | tf_op jit(solution)/shard_map/all_gather | solution.py:63
  200.8 11.1 %all-to-all-start = ((f32[32,1,256]{2,1,0:T(1,128)}), f32[32,1,256]{2,1,0:T(1,128)S(1)}, u32[]{:S(2)}, u32[]{:S(2)}) async-start(f32[32,1,256]{2,1,0:T(1,128)} %all_to_all.30), calls=%async_computation | async-start | bytes 65536 | tf_op jit(solution)/shard_map/all_to_all | solution.py:69
  211.9 11.2 %all-to-all-start.1 = ((f32[32,1,256]{2,1,0:T(1,128)}), f32[32,1,256]{2,1,0:T(1,128)S(1)}, u32[]{:S(2)}, u32[]{:S(2)}) async-start(f32[32,1,256]{2,1,0:T(1,128)} %all_to_all.32), calls=%async_computation.1 | async-start | bytes 65536 | tf_op jit(solution)/shard_map/all_to_all | solution.py:70
  223.1 11.3 %all-to-all-start.2 = ((f32[32,1,256]{2,1,0:T(1,128)}), f32[32,1,256]{2,1,0:T(1,128)S(1)}, u32[]{:S(2)}, u32[]{:S(2)}) async-start(f32[32,1,256]{2,1,0:T(1,128)} %all_to_all.36), calls=%async_computation.2 | async-start | bytes 65536 | tf_op jit(solution)/shard_map/all_to_all | solution.py:71
  234.4 30.0 %all-to-all-start.3 = ((f32[32,1,256]{2,1,0:T(1,128)}), f32[32,1,256]{2,1,0:T(1,128)S(1)}, u32[]{:S(2)}, u32[]{:S(2)}) async-start(f32[32,1,256]{2,1,0:T(1,128)} %all_to_all.39), calls=%async_computation.3 | async-start | bytes 65536 | tf_op jit(solution)/shard_map/all_to_all | solution.py:72
Sparse Core Ops, SparseCore 0:
  11.6 116.1 all-gather.10
where the time goes:
time: 284 us
  waiting for transfers between devices  105 us (37%)
  blocking collectives  58.3 us (21%)
  matrix products  55.4 us (20%)
  starting transfers between devices  22.9 us (8%)
  other arithmetic  17.6 us (6%)
  between operations  16.6 us (6%)
  local copies, waits for them, and re-layouts  6.78 us (2%)
    all_gather x1, waiting for transfers between devices, per_device(): block = lax.all_gather(normed, 'req', axis=0, tiled=True)  91 us
    dot_general x16, matrix products, block_stats(): logits = jnp.dot(block, matrix, preferred_element_type=jnp.float32)  55.4 us
    all_gather x4, blocking collectives, combined_all(): everything = jax.tree.map(lambda part: lax.all_gather(part, axis), value)  33.2 us
    all_gather x1, blocking collectives, per_device(): target = lax.all_gather(target_ids, 'req', axis=0, tiled=True)  25.2 us
    reduce_sum x16, other arithmetic, block_stats(): weighted = jnp.sum(shifted * logits, axis=-1)  11.5 us
    all_to_all x1, starting transfers between devices, per_device(): lax.all_to_all(shaped[2], 'req', split_axis=0, concat_axis=0, tiled=True)  5.79 us
    all_to_all x1, starting transfers between devices, per_device(): lax.all_to_all(shaped[3], 'req', split_axis=0, concat_axis=0, tiled=True)  5.77 us
    all_to_all x1, starting transfers between devices, per_device(): lax.all_to_all(shaped[1], 'req', split_axis=0, concat_axis=0, tiled=True)  5.72 us
  transfers between devices with their start and end apart: 5, of which 4 were waited for; matrix products, arithmetic and copies ran while one was open for 0% of the time, Pallas kernels for 0%

commit v1 on v0

--- a/solution.py
+++ b/solution.py
@@ -60,7 +60,9 @@
     vbase = (my_req * n_tp + lax.axis_index("tp")) * vdev
     columns = lax.broadcasted_iota(jnp.int32, (1, vdev), 1)
     own_vocab = columns + vbase
-    block = lax.all_gather(normed, "req", axis=0, tiled=True)
+    block = jnp.concatenate(
+        lax.all_to_all(jnp.stack([normed] * lax.axis_size("req")), "req", 0, 0), axis=0
+    )
     target = lax.all_gather(target_ids, "req", axis=0, tiled=True)
     stats = blocked_stats(block, target, head, own_vocab)
     gathered = tuple((new for new in stats))

time: 284 us -> 735 us (2.59)
  blocking collectives: 58.3 us -> 595 us
  waiting for transfers between devices: 105 us -> 13.9 us
  between operations: 16.6 us -> 3.22 us
  local copies, waits for them, and re-layouts: 6.78 us -> 17.8 us
  starting transfers between devices: 22.9 us -> 31.7 us
    all_gather x1, blocking collectives: 25.2 us -> 562 us  [per_device(): target = lax.all_gather(target_ids, 'req', axis=0, tiled=True)]
    all_gather x1 -> x0, waiting for transfers between devices: 91 us -> none  [per_device(): block = lax.all_gather(normed, 'req', axis=0, tiled=True)]
    another operation x0 -> x1, local copies, waits for them, and re-layouts: none -> 11 us  [per_device(): jnp.stack([normed] * lax.axis_size('req'))]
    all_to_all x0 -> x1, starting transfers between devices: none -> 8.77 us  [per_device(): lax.all_to_all(jnp.stack([normed] * lax.axis_size('req')), 'req', 0, 0)]
  transfers between devices with their start and end apart: 5 -> 5, of which waited for: 4 -> 3; matrix products, arithmetic and copies ran while one was open for 0% -> 0% of each run, Pallas kernels for 0% -> 0%
where the time goes in v1:
time: 735 us; the launch traced here: 734 us
  blocking collectives  595 us (81%)
  matrix products  55.4 us (8%)
  starting transfers between devices  31.7 us (4%)
  local copies, waits for them, and re-layouts  17.8 us (2%)
  other arithmetic  16.4 us (2%)
  waiting for transfers between devices  13.9 us (2%)
    all_gather x1, blocking collectives, per_device(): target = lax.all_gather(target_ids, 'req', axis=0, tiled=True)  562 us
    dot_general x16, matrix products, block_stats(): logits = jnp.dot(block, matrix, preferred_element_type=jnp.float32)  55.4 us
    all_gather x4, blocking collectives, combined_all(): everything = jax.tree.map(lambda part: lax.all_gather(part, axis), value)  33.3 us
  transfers between devices with their start and end apart: 5, of which 3 were waited for; matrix products, arithmetic and copies ran while one was open for 0% of the time, Pallas kernels for 0%

profile of v1, /device:TPU:14, one launch (start us, length us, event | category | flops | bytes accessed | tf_op | source)
XLA Modules:
  0.0 734.4 jit_solution(10193787667716911730)
XLA Ops:
  3.7 11.0 %stack.2 = bf16[32,256,2048]{2,1,0:T(8,128)(2,1)} broadcast(bf16[256,2048]{1,0:T(8,128)(2,1)S(1)} %fusion.9), dimensions={1,2} | broadcast | bytes 34603008 | tf_op jit(solution)/shard_map/stack | solution.py:64
  14.7 8.8 %all-to-all-start = ((bf16[32,256,2048]{2,1,0:T(8,128)(2,1)}), bf16[32,256,2048]{2,1,0:T(8,128)(2,1)}, u32[]{:S(2)}, u32[]{:S(2)}) async-start(bf16[32,256,2048]{2,1,0:T(8,128)(2,1)} %stack.2), calls=%async_computation | async-start | bytes 67108864 | tf_op jit(solution)/shard_map/all_to_all | solution.py:64
  23.6 561.7 %all-gather.4 = s32[32,1,256]{2,1,0:T(1,128)S(1)} all-gather(s32[1,1,256]{2,1,0:T(1,128)S(1)} %bitcast.102), channel_id=1, replica_groups=mesh['req'=32,'tp'=4] {'req'}, dimensions={0}, use_global_device_ids=true | all-gather | bytes 33792 | tf_op jit(solution)/shard_map/all_gather | solution.py:66
  585.3 72.2 %while.39 = (s32[]{:T(128)}, f32[16,512]{1,0:T(8,128)S(1)}, f32[16,512]{1,0:T(8,128)S(1)}, f32[16,512]{1,0:T(8,128)S(1)}, f32[16,512]{1,0:T(8,128)S(1)}, /*index...) while((s32[]{:T(128)}, f32[16,512]{1,0:T(8,128)S(1)}, ...), condition=%wide.region_6.7_spmd.clone, body=%wide.region_1.6_spmd.clone.sunk | while | flops 1613757184 | bytes 8428165 | solution.py:44
  585.3 3.5 fusion.19
  589.9 3.5 fusion.19
  594.4 3.5 fusion.19
  598.9 3.5 fusion.19
  603.4 3.5 fusion.19
  612.4 3.5 fusion.19
  630.5 3.5 fusion.19
  635.0 3.5 fusion.19
  653.1 3.5 fusion.19
  658.2 5.6 all-to-all-start.1
  664.5 4.9 all-to-all-done.1
  669.4 5.7 all-to-all-start.2
  675.7 4.8 all-to-all-done.2
  680.6 5.8 all-to-all-start.3
  687.7 4.1 all-to-all-done.3
  691.9 5.8 all-to-all-start.4
  697.7 7.9 %all-gather.6 = f32[4,1,256]{2,1,0:T(1,128)S(1)} all-gather(f32[1,1,256]{2,1,0:T(1,128)S(1)} %bitcast.100), channel_id=3, replica_groups=mesh['req'=32,'tp'=4] {'tp'}, dimensions={0}, use_global_device_ids=true | all-gather | bytes 5120 | tf_op jit(solution)/shard_map/all_gather | solution.py:9
  705.6 9.4 %all-gather.7 = f32[4,1,256]{2,1,0:T(1,128)S(1)} all-gather(f32[1,1,256]{2,1,0:T(1,128)S(1)} %bitcast.99), channel_id=4, replica_groups=mesh['req'=32,'tp'=4] {'tp'}, dimensions={0}, use_global_device_ids=true | all-gather | bytes 5120 | tf_op jit(solution)/shard_map/all_gather | solution.py:9
  715.1 7.0 all-gather.5
  722.1 9.0 %all-gather.8 = f32[4,1,256]{2,1,0:T(1,128)S(1)} all-gather(f32[1,1,256]{2,1,0:T(1,128)S(1)} %bitcast.101), channel_id=5, replica_groups=mesh['req'=32,'tp'=4] {'tp'}, dimensions={0}, use_global_device_ids=true | all-gather | bytes 5120 | tf_op jit(solution)/shard_map/all_gather | solution.py:9
  (169 shorter events, 47.7 us)
Async XLA Ops:
  14.7 8.8 %copy-start = (s32[256]{0:T(256)S(1)}, s32[256]{0:T(256)}, u32[]{:S(2)}) copy-start(s32[256]{0:T(256)} %param.12) | copy-start | bytes 3076
  14.7 570.6 %copy-start.1 = (bf16[2048,768]{1,0:T(8,128)(2,1)S(1)}, bf16[2048,768]{1,0:T(8,128)(2,1)}, u32[]{:S(2)}) copy-start(bf16[2048,768]{1,0:T(8,128)(2,1)} %param.11) | copy-start | bytes 9437188
  14.7 570.6 %all-to-all-start = ((bf16[32,256,2048]{2,1,0:T(8,128)(2,1)}), bf16[32,256,2048]{2,1,0:T(8,128)(2,1)}, u32[]{:S(2)}, u32[]{:S(2)}) async-start(bf16[32,256,2048]{2,1,0:T(8,128)(2,1)} %stack.2), calls=%async_computation | async-start | bytes 67108864 | tf_op jit(solution)/shard_map/all_to_all | solution.py:64
  658.2 11.1 %all-to-all-start.1 = ((f32[32,1,256]{2,1,0:T(1,128)}), f32[32,1,256]{2,1,0:T(1,128)S(1)}, u32[]{:S(2)}, u32[]{:S(2)}) async-start(f32[32,1,256]{2,1,0:T(1,128)} %all_to_all.34), calls=%async_computation.1 | async-start | bytes 65536 | tf_op jit(solution)/shard_map/all_to_all | solution.py:71
  669.4 11.2 %all-to-all-start.2 = ((f32[32,1,256]{2,1,0:T(1,128)}), f32[32,1,256]{2,1,0:T(1,128)S(1)}, u32[]{:S(2)}, u32[]{:S(2)}) async-start(f32[32,1,256]{2,1,0:T(1,128)} %all_to_all.36), calls=%async_computation.2 | async-start | bytes 65536 | tf_op jit(solution)/shard_map/all_to_all | solution.py:72
  680.6 11.3 %all-to-all-start.3 = ((f32[32,1,256]{2,1,0:T(1,128)}), f32[32,1,256]{2,1,0:T(1,128)S(1)}, u32[]{:S(2)}, u32[]{:S(2)}) async-start(f32[32,1,256]{2,1,0:T(1,128)} %all_to_all.40), calls=%async_computation.3 | async-start | bytes 65536 | tf_op jit(solution)/shard_map/all_to_all | solution.py:73
  691.9 30.2 %all-to-all-start.4 = ((f32[32,1,256]{2,1,0:T(1,128)}), f32[32,1,256]{2,1,0:T(1,128)S(1)}, u32[]{:S(2)}, u32[]{:S(2)}) async-start(f32[32,1,256]{2,1,0:T(1,128)} %all_to_all.43), calls=%async_computation.4 | async-start | bytes 65536 | tf_op jit(solution)/shard_map/all_to_all | solution.py:74
